TPU v7x, 32 devices: a whole 2x2x4 slice. The times are simulated.
32 devices in a mesh: gx: 4 (over z), gy: 8 (over y, x, core).
Axes of the slice: x: 2, y: 2, z: 4, core: 2. Of those that a mesh axis runs over, the one named last changes fastest.
Arguments:
- initial_field: float32 [8, 32, 2048], P(None, 'gx', 'gy'), may hold values from -6 to 6
- target_field: float32 [8, 32, 2048], P(None, 'gx', 'gy'), may hold values from -8 to 8
- land_mask: int32 [32, 2048], P('gx', 'gy'), may hold values 0 or 1
- conv_one: float32 [64, 73], replicated, may hold values from -0.75 to 0.75
- conv_two: float32 [64, 577], replicated, may hold values from -0.25 to 0.25
- head_weights: float32 [32, 65], replicated, may hold values from -0.75 to 0.75
- dir_one: float32 [64, 73], replicated, may hold values from -6 to 6
- dir_two: float32 [64, 577], replicated, may hold values from -6 to 6
- dir_three: float32 [32, 65], replicated, may hold values from -6 to 6
- group_ids: int32 [160], replicated, may hold values from 0 to 5, as said below
Outputs:
- final_field: float32 [8, 32, 2048], P(None, 'gx', 'gy')
- update_one: float32 [64, 73], replicated
- update_two: float32 [64, 577], replicated
- update_three: float32 [32, 65], replicated
Inputs may be any that keep to these rules, and one draw needn't show every extreme that they name: `group_ids`: each of the 6 group numbers names 26 or 27 rows.
All inputs are finite; a program needn't handle non-finite values. No bound on the sum of `land_mask` on one device may be relied on, other than what follows from the above.
Results may differ from a plain program's by a relative error of at most 0.0024.
The roundings to bfloat16 on the way count: a program that leaves them out, or rounds other values in their place, can miss the bound.
Values may be sent and summed in bfloat16 or wider, within the bound.
A program may use at most 64 MiB of HBM per device.

v0:
```python
import functools
import math

import jax
import jax.numpy as jnp
from jax import lax
from jax.experimental import pallas as pl
from jax.experimental.pallas import tpu as pltpu
from jax.sharding import PartitionSpec as P

GROUPS = 6
PARAMS = 43680
RIM = 6
LEV = 8
C = 64
K = 32
TILE = 128
MESH = pl.DeviceIdType.MESH
F32 = jnp.float32
BF16 = jnp.bfloat16
VM = pl.BlockSpec(memory_space=pltpu.VMEM)
LIMIT = 56 * 1024 * 1024
NT = (((1,), (1,)), ((), ()))


def dot(a, b):
    return jnp.dot(a, b, preferred_element_type=F32)


def dot_nt(a, b):
    return lax.dot_general(a, b, NT, preferred_element_type=F32)


def sigmoid(v):
    return 0.5 * jnp.tanh(0.5 * v) + 0.5


def halo_kernel(sizes, field, target, mask, own, left, right, send_sem, recv_sem):
    n_gx, n_gy = sizes
    gx = lax.axis_index("gx")
    gy = lax.axis_index("gy")
    h, width = mask.shape
    for r in range(h):
        wet = jnp.broadcast_to(mask[r : r + 1, :].astype(F32), (LEV, width))
        own[RIM + r, 0:8, :] = wet * field[:, r, :]
        own[RIM + r, 8:16, :] = wet
        own[RIM + r, 16:24, :] = target[:, r, :]

    middle = pl.ds(RIM, h)
    top = pl.ds(0, RIM)
    bottom = pl.ds(RIM + h, RIM)
    first = pl.ds(RIM, RIM)
    last = pl.ds(h, RIM)
    all_lanes = pl.ds(0, width)
    low = pl.ds(0, TILE)
    high = pl.ds(width - TILE, TILE)
    rows_of = {1: (last, top), 0: (middle, middle), -1: (first, bottom)}
    lanes_of = {1: (high, left, low), 0: (all_lanes, own, all_lanes), -1: (low, right, low)}
    moves = [(dx, dy) for dx in (-1, 0, 1) for dy in (-1, 0, 1) if (dx, dy) != (0, 0)]

    def exists(dx, dy):
        x = gx + dx
        y = gy + dy
        return (x >= 0) & (x < n_gx) & (y >= 0) & (y < n_gy)

    barrier = pltpu.get_barrier_semaphore()
    count = jnp.int32(0)
    for dx, dy in moves:
        @pl.when(exists(dx, dy))
        def _():
            pl.semaphore_signal(barrier, inc=1, device_id=(gx + dx, gy + dy), device_id_type=MESH)
        count = count + jnp.where(exists(dx, dy), 1, 0)
    for dx, dy in moves:
        @pl.when(jnp.logical_not(exists(-dx, -dy)))
        def _():
            _, dst_rows = rows_of[dx]
            _, dst, dst_lanes = lanes_of[dy]
            dst[dst_rows, :, dst_lanes] = jnp.zeros((dst_rows.size, 24, dst_lanes.size), F32)
    pl.semaphore_wait(barrier, count)

    copies = []
    for index, (dx, dy) in enumerate(moves):
        src_rows, dst_rows = rows_of[dx]
        src_lanes, dst, dst_lanes = lanes_of[dy]
        copies.append(
            pltpu.make_async_remote_copy(
                src_ref=own.at[src_rows, :, src_lanes],
                dst_ref=dst.at[dst_rows, :, dst_lanes],
                send_sem=send_sem.at[index],
                recv_sem=recv_sem.at[index],
                device_id=(gx + dx, gy + dy),
                device_id_type=MESH,
            )
        )
    for (dx, dy), copy in zip(moves, copies):
        @pl.when(exists(dx, dy))
        def _():
            copy.start()
    for (dx, dy), copy in zip(moves, copies):
        @pl.when(exists(-dx, -dy))
        def _():
            copy.wait_recv()
    for (dx, dy), copy in zip(moves, copies):
        @pl.when(exists(dx, dy))
        def _():
            copy.wait_send()


def roll(v, shift):
    return pltpu.roll(v, shift % v.shape[1], 1)


def compute_kernel(
    sizes, own, left, right, w1_ref, w2_ref, w3_ref,
    final_ref, grads_ref,
    fld, wet_s, tgt, adj, x9, z1, h1, z2, h2, prob, e2m, up, e1m, vv, e3m,
):
    n_gx, n_gy = sizes
    gx = lax.axis_index("gx")
    gy = lax.axis_index("gy")
    rows, _, width = own.shape
    h = rows - 2 * RIM
    wide = width + TILE

    lane = lax.broadcasted_iota(jnp.int32, (LEV, TILE), 1)
    is_right = lane < TILE // 2

    def merge(r, _):
        rest = jnp.where(is_right, right[r, 0:8, :], left[r, 0:8, :])
        fld[0, r] = jnp.concatenate([own[r, 0:8, :], rest], axis=1)
        rest = jnp.where(is_right, right[r, 8:16, :], left[r, 8:16, :])
        wet_s[r] = jnp.concatenate([own[r, 8:16, :], rest], axis=1)
        rest = jnp.where(is_right, right[r, 16:24, :], left[r, 16:24, :])
        tgt[r] = jnp.concatenate([own[r, 16:24, :], rest], axis=1)
        return 0

    lax.fori_loop(0, rows, merge, 0)

    wa = w1_ref[...]
    w1 = wa[:, : 9 * LEV].astype(BF16)
    b1 = wa[:, 9 * LEV :]
    wb = w2_ref[...]
    tap = lambda a, b: wb[:, (3 * a + b) * C : (3 * a + b + 1) * C]
    w2f = jnp.concatenate(
        [jnp.concatenate([tap(a, b) for a in range(3)], axis=1) for b in range(3)], axis=0
    )
    w2 = w2f.astype(BF16)
    w2t = w2f.T.astype(BF16)
    b2 = wb[:, 9 * C :]
    wc = w3_ref[...]
    w3 = wc[:, :C].astype(BF16)
    w3t = wc[:, :C].T.astype(BF16)
    b3 = wc[:, C:]
    w1t = wa[:, : 9 * LEV].T.astype(BF16)

    col_left = jnp.where(gy > 0, 1.0, 0.0).astype(F32)
    col_right = jnp.where(gy < n_gy - 1, 1.0, 0.0).astype(F32)
    side = jnp.where(is_right[0:1], col_right, col_left)
    col_ok = jnp.concatenate([jnp.ones((1, width), F32), side], axis=1)

    def inside(r):
        i = gx * h + r - RIM
        ok = (i >= 0) & (i < n_gx * h)
        return col_ok * jnp.where(ok, 1.0, 0.0).astype(F32)

    def loop(start, stop, body, unroll):
        lax.fori_loop(start, stop, lambda r, c: (body(r), c)[1], 0, unroll=unroll)

    def forward(s, rad):
        def first(r):
            parts = []
            for a in range(3):
                row = fld[s, r + a - 1]
                parts += [roll(row, 1), row, roll(row, -1)]
            cols = jnp.concatenate(parts, axis=0).astype(BF16)
            x9[s, r] = cols
            z = dot(w1, cols) + b1
            z1[s, r] = z
            h1[s, r] = (z * sigmoid(z) * inside(r)).astype(BF16)

        loop(RIM - rad - 1, RIM + h + rad + 1, first, 2)

        def second(r):
            h3 = jnp.concatenate([h1[s, r - 1], h1[s, r], h1[s, r + 1]], axis=0)
            y = dot(w2, h3)
            z = roll(y[0:C], 1) + y[C : 2 * C] + roll(y[2 * C :], -1) + b2
            z2[s, r] = z
            hb = (z * sigmoid(z)).astype(BF16)
            h2[s, r] = hb
            p = sigmoid(dot(w3, hb) + b3)
            prob[s, r] = p
            center = fld[s, r]
            c = 0.25 * p
            change = (
                c[0:8] * (fld[s, r + 1] - center)
                + c[8:16] * (fld[s, r - 1] - center)
                + c[16:24] * (roll(center, -1) - center)
                + c[24:32] * (roll(center, 1) - center)
            )
            fld[s + 1, r] = center + wet_s[r] * change

        loop(RIM - rad, RIM + h + rad, second, 2)

    forward(0, 4)
    forward(1, 2)
    for r in range(h):
        final_ref[:, r, :] = fld[2, RIM + r][:, :width]

    def adjoint_start(r):
        adj[1, r] = wet_s[r] * (fld[2, r] - tgt[r])

    loop(RIM - 2, RIM + h + 2, adjoint_start, 1)

    lane_w = lax.broadcasted_iota(jnp.int32, (1, wide), 1)
    own_lane = jnp.where(lane_w < width, 1.0, 0.0).astype(F32)
    fold = lambda v: sum(v[:, k * TILE : (k + 1) * TILE] for k in range(v.shape[1] // TILE))

    def errors(s, r):
        center = fld[s, r]
        wg = wet_s[r] * adj[s, r]
        p = prob[s, r]
        diff = jnp.concatenate(
            [
                wg * (fld[s, r + 1] - center),
                wg * (fld[s, r - 1] - center),
                wg * (roll(center, -1) - center),
                wg * (roll(center, 1) - center),
            ],
            axis=0,
        )
        e3 = diff * (0.25 * p * (1.0 - p))
        e3b = e3.astype(BF16)
        z = z2[s, r]
        g = sigmoid(z)
        e2 = dot(w3t, e3b) * (g * (1.0 + z * (1.0 - g)))
        return e3, e3b, e2

    def spread(e2):
        return jnp.concatenate([roll(e2, -1), e2, roll(e2, 1)], axis=0).astype(BF16)

    zero_b = (jnp.zeros((K, TILE), F32), jnp.zeros((C, TILE), F32))

    def own_rows(s, carry):
        def body(r, c):
            e3, e3b, e2 = errors(s, r)
            e3m[s, r - RIM] = e3b[:, :width]
            em = e2 * own_lane
            m = spread(em)
            e2m[s, r - RIM] = m
            if s == 0:
                up[r] = dot(w2t, m)
            else:
                up[r] = dot(w2t, spread(e2))
            return (c[0] + fold(e3[:, :width]), c[1] + fold(e2[:, :width]))

        return lax.fori_loop(RIM, RIM + h, body, carry, unroll=2)

    def rim_row(r):
        _, _, e2 = errors(1, r)
        up[r] = dot(w2t, spread(e2))

    def first_error(s, r):
        hid = up[r + 1][0:C] + up[r][C : 2 * C] + up[r - 1][2 * C :]
        z = z1[s, r]
        g = sigmoid(z)
        return hid * (g * (1.0 + z * (1.0 - g))) * inside(r)

    sums = own_rows(1, zero_b)
    for r in (RIM - 2, RIM - 1, RIM + h, RIM + h + 1):
        rim_row(r)

    def back_one(r, c):
        e1 = first_error(1, r)
        eb = e1.astype(BF16)
        e1m[1, r - RIM + 1] = (e1 * own_lane).astype(BF16)
        t = dot(w1t, eb)
        piece = lambda a, b: t[(3 * a + b) * LEV : (3 * a + b + 1) * LEV]
        for a in range(3):
            vv[r, a] = roll(piece(a, 0), -1) + piece(a, 1) + roll(piece(a, 2), 1)
        keep = jnp.where((r >= RIM) & (r < RIM + h), 1.0, 0.0).astype(F32)
        return c + fold(e1[:, :width]) * keep

    sum_one = lax.fori_loop(
        RIM - 1, RIM + h + 1, back_one, jnp.zeros((C, TILE), F32), unroll=2
    )

    def adjoint_next(r):
        wg = wet_s[r] * adj[1, r]
        p = prob[1, r]
        c = [0.25 * p[n * 8 : n * 8 + 8] for n in range(4)]
        above = wet_s[r - 1] * adj[1, r - 1] * (0.25 * prob[1, r - 1][0:8])
        below = wet_s[r + 1] * adj[1, r + 1] * (0.25 * prob[1, r + 1][8:16])
        adj[0, r] = (
            adj[1, r]
            - wg * (c[0] + c[1] + c[2] + c[3])
            + above
            + below
            + roll(wg * c[2], 1)
            + roll(wg * c[3], -1)
            + vv[r + 1, 0]
            + vv[r, 1]
            + vv[r - 1, 2]
        )

    loop(RIM, RIM + h, adjoint_next, 1)

    sums = own_rows(0, sums)
    for r in (RIM - 2, RIM - 1, RIM + h, RIM + h + 1):
        up[r] = jnp.zeros((3 * C, wide), F32)

    def back_zero(r, c):
        e1 = first_error(0, r)
        e1m[0, r - RIM + 1] = e1.astype(BF16)
        return c + fold(e1)

    sum_one = lax.fori_loop(RIM - 1, RIM + h + 1, back_zero, sum_one, unroll=2)

    g1 = jnp.zeros((C, 9 * LEV), F32)
    g2 = jnp.zeros((3 * C, 3 * C), F32)
    g3 = jnp.zeros((K, C), F32)
    for s in range(2):
        for r in range(h):
            h3 = jnp.concatenate([h1[s, RIM + r + a - 1] for a in range(3)], axis=0)
            g2 = g2 + dot_nt(e2m[s, r], h3)
            g3 = g3 + dot_nt(e3m[s, r], h2[s, RIM + r][:, :width])
        for r in range(h + 2) if s == 0 else range(1, h + 1):
            g1 = g1 + dot_nt(e1m[s, r], x9[s, RIM + r - 1])
    total = lambda v: jnp.sum(v, axis=1, keepdims=True)
    pad = lambda v: jnp.concatenate([v, jnp.zeros((v.shape[0], C - v.shape[1]), F32)], axis=1)
    extra = jnp.concatenate(
        [
            g1[:, :C],
            pad(jnp.concatenate([g1[:, C:], total(sum_one), total(sums[1])], axis=1)),
            g3,
            pad(total(sums[0])),
        ],
        axis=0,
    )
    grads_ref[: 3 * C, :] = jnp.concatenate([g2, extra], axis=1)
    spare = grads_ref.shape[0] - 3 * C
    if spare:
        grads_ref[3 * C :, :] = jnp.zeros((spare, 4 * C), F32)


def sum_kernel(sizes, grads, out, got, part, parts, send_one, recv_one, send_two, recv_two,
               send_three, recv_three):
    n_gx, n_gy = sizes
    gx = lax.axis_index("gx")
    gy = lax.axis_index("gy")
    chunk = grads.shape[0] // n_gy
    barrier = pltpu.get_barrier_semaphore()
    ys = [lax.rem(gy + k, n_gy) for k in range(1, n_gy)]
    xs = [lax.rem(gx + k, n_gx) for k in range(1, n_gx)]
    for y in ys:
        pl.semaphore_signal(barrier, inc=1, device_id=(gx, y), device_id_type=MESH)
    for x in xs:
        pl.semaphore_signal(barrier, inc=1, device_id=(x, gy), device_id_type=MESH)
    pl.semaphore_wait(barrier, n_gy + n_gx - 2)

    def rows(y):
        return pl.ds(pl.multiple_of(y * chunk, 8), chunk)

    one = [
        pltpu.make_async_remote_copy(
            src_ref=grads.at[rows(y)], dst_ref=got.at[k],
            send_sem=send_one.at[k], recv_sem=recv_one.at[k],
            device_id=(gx, y), device_id_type=MESH,
        )
        for k, y in enumerate(ys)
    ]
    for copy in one:
        copy.start()
    acc = grads[rows(gy), :]
    for k, copy in enumerate(one):
        copy.wait_recv()
        acc = acc + got[k]
    part[...] = acc
    two = [
        pltpu.make_async_remote_copy(
            src_ref=part, dst_ref=parts.at[gx],
            send_sem=send_two.at[k], recv_sem=recv_two.at[k],
            device_id=(x, gy), device_id_type=MESH,
        )
        for k, x in enumerate(xs)
    ]
    for copy in two:
        copy.start()
    parts[gx] = acc
    for copy in two:
        copy.wait_recv()
    acc = parts[0]
    for x in range(1, n_gx):
        acc = acc + parts[x]
    out[rows(gy), :] = acc
    three = [
        pltpu.make_async_remote_copy(
            src_ref=out.at[rows(gy)], dst_ref=out.at[rows(gy)],
            send_sem=send_three.at[k], recv_sem=recv_three.at[k],
            device_id=(gx, y), device_id_type=MESH,
        )
        for k, y in enumerate(ys)
    ]
    for copy in three:
        copy.start()
    for copy in three:
        copy.wait_recv()
    for copy in one + two + three:
        copy.wait_send()


def finish_kernel(grads, d1, d2, d3, ids, u1, u2, u3):
    g = grads[: 3 * C, :]
    block = lambda a, b: g[b * C : (b + 1) * C, a * C : (a + 1) * C]
    side = g[:, 3 * C :]
    one = jnp.concatenate([side[:C], side[C : 2 * C, : 9 * LEV - C + 1]], axis=1)
    bias_two = side[C : 2 * C, 9 * LEV - C + 1 : 9 * LEV - C + 2]
    two = jnp.concatenate([block(a, b) for a in range(3) for b in range(3)] + [bias_two], axis=1)
    three = jnp.concatenate([side[2 * C : 2 * C + K], side[2 * C + K :, 0:1]], axis=1)
    members = [one, two, three]
    heads = [d1[...], d2[...], d3[...]]
    row_sq = lambda v: jnp.sum(v * v, axis=1, keepdims=True)
    grad_rows = jnp.concatenate([row_sq(m) for m in members], axis=0)
    dir_rows = jnp.concatenate([row_sq(m) for m in heads], axis=0)
    total = jnp.sum(grad_rows, axis=0, keepdims=True)
    factor = 1.0 / jnp.maximum(jnp.sqrt(total), 1.0)
    clip_rows = grad_rows * (factor * factor)
    count = grad_rows.shape[0]
    i0 = lax.broadcasted_iota(jnp.int32, (count, count), 0)
    i1 = lax.broadcasted_iota(jnp.int32, (count, count), 1)
    spread = jnp.broadcast_to(ids[...].astype(F32), (count, count))
    column = jnp.sum(jnp.where(i0 == i1, spread, 0.0), axis=1, keepdims=True)
    row_ratio = jnp.zeros((count, 1), F32)
    for k in range(GROUPS):
        hit = column == float(k)
        pick = lambda v: jnp.sum(jnp.where(hit, v, 0.0), axis=0, keepdims=True)
        ratio = jnp.sqrt(pick(clip_rows)) / jnp.sqrt(pick(dir_rows) + 1e-06)
        row_ratio = row_ratio + jnp.where(hit, ratio, 0.0)
    scaling = math.sqrt(PARAMS)
    start = 0
    for ref, member, head in zip((u1, u2, u3), members, heads):
        n = member.shape[0]
        ref[...] = scaling * (member * factor + row_ratio[start : start + n] * head)
        start += n


def per_device(sizes, field, target, mask, conv_one, conv_two, head, d1, d2, d3, ids):
    n_gx, n_gy = sizes
    _, h, width = field.shape
    rows = h + 2 * RIM
    wide = width + TILE
    shape = jax.ShapeDtypeStruct
    chunk = 8 * -(-3 * C // (8 * n_gy))
    own, left, right = pl.pallas_call(
        functools.partial(halo_kernel, sizes),
        name="halo",
        out_shape=[
            shape((rows, 24, width), F32),
            shape((rows, 24, TILE), F32),
            shape((rows, 24, TILE), F32),
        ],
        in_specs=[VM] * 3,
        out_specs=[VM] * 3,
        scratch_shapes=[pltpu.SemaphoreType.DMA((8,)), pltpu.SemaphoreType.DMA((8,))],
        compiler_params=pltpu.CompilerParams(collective_id=0, has_side_effects=True),
    )(field, target, mask)
    final, grads = pl.pallas_call(
        functools.partial(compute_kernel, sizes),
        name="local",
        out_shape=[shape(field.shape, F32), shape((chunk * n_gy, 4 * C), F32)],
        in_specs=[VM] * 6,
        out_specs=[VM] * 2,
        scratch_shapes=[
            pltpu.VMEM((3, rows, LEV, wide), F32),
            pltpu.VMEM((rows, LEV, wide), F32),
            pltpu.VMEM((rows, LEV, wide), F32),
            pltpu.VMEM((2, rows, LEV, wide), F32),
            pltpu.VMEM((2, rows, 9 * LEV, wide), BF16),
            pltpu.VMEM((2, rows, C, wide), F32),
            pltpu.VMEM((2, rows, C, wide), BF16),
            pltpu.VMEM((2, rows, C, wide), F32),
            pltpu.VMEM((2, rows, C, wide), BF16),
            pltpu.VMEM((2, rows, K, wide), F32),
            pltpu.VMEM((2, h, 3 * C, wide), BF16),
            pltpu.VMEM((rows, 3 * C, wide), F32),
            pltpu.VMEM((2, h + 2, C, wide), BF16),
            pltpu.VMEM((rows, 3, LEV, wide), F32),
            pltpu.VMEM((2, h, K, width), BF16),
        ],
        compiler_params=pltpu.CompilerParams(vmem_limit_bytes=LIMIT),
    )(own, left, right, conv_one, conv_two, head)
    dma = pltpu.SemaphoreType.DMA
    summed = pl.pallas_call(
        functools.partial(sum_kernel, sizes),
        name="gradsum",
        out_shape=shape(grads.shape, F32),
        in_specs=[VM],
        out_specs=VM,
        scratch_shapes=[
            pltpu.VMEM((n_gy - 1, chunk, 4 * C), F32),
            pltpu.VMEM((chunk, 4 * C), F32),
            pltpu.VMEM((n_gx, chunk, 4 * C), F32),
            dma((n_gy - 1,)), dma((n_gy - 1,)),
            dma((n_gx - 1,)), dma((n_gx - 1,)),
            dma((n_gy - 1,)), dma((n_gy - 1,)),
        ],
        compiler_params=pltpu.CompilerParams(collective_id=1, has_side_effects=True),
    )(grads)
    u1, u2, u3 = pl.pallas_call(
        finish_kernel,
        name="update",
        out_shape=[shape(conv_one.shape, F32), shape(conv_two.shape, F32), shape(head.shape, F32)],
        in_specs=[VM] * 5,
        out_specs=[VM] * 3,
    )(summed, d1, d2, d3, ids.reshape(1, -1))
    return final, u1, u2, u3


def solution(mesh):
    grid = P(None, "gx", "gy")
    placed = (grid, grid, P("gx", "gy")) + (P(),) * 7
    return jax.shard_map(
        functools.partial(per_device, (mesh.shape["gx"], mesh.shape["gy"])),
        mesh=mesh,
        in_specs=placed,
        out_specs=(grid, P(), P(), P()),
        check_vma=False,
    )
```

profile of v0, /device:TPU:0, one launch (start us, length us, event | category | flops | bytes accessed | tf_op | source)
XLA Modules:
  0.0 63.3 jit_solution(15591789113191809972)
XLA Ops:
  0.6 11.0 %halo.1 = (f32[20,24,256]{2,1,0:T(8,128)}, f32[20,24,128]{2,1,0:T(8,128)}, f32[20,24,128]{2,1,0:T(8,128)}) custom-call(f32[8,8,256]{2,1,0:T(8,128)} %field.1, f32[8,8,256]{2,1,0:T(8,128)} %target.1, s32[8,256]{1,0:T(8,128)} %mask.1), custom_call_target="tpu_custom_call" | custom-call | tf_op jit(solution)/shard_map/halo/pallas_call | solution.py:453
  11.6 29.2 %local.1 = (f32[8,8,256]{2,1,0:T(8,128)}, f32[192,256]{1,0:T(8,128)}) custom-call(f32[20,24,256]{2,1,0:T(8,128)} %get-tuple-element.12.own, f32[20,24,128]{2,1,0:T(8,128)} %get-tuple-element.13.left, f32[20,24,128]{2,1,0:T(8,128)} %get-tuple-element.14.right, f32[64,73]{1,0:T(8,128)} %w1_ref.1, f32[64,577]{1,0:T(8,128)} %w2_ref.1, f32[32,65]{1,0:T(8,128)} %w3_ref.1), custom_call_target="tpu_custom_call" | custom-call | tf_op jit(solution)/shard_map/local/pallas_call | solution.py:466
  40.9 20.2 %gradsum.1.grads = f32[192,256]{1,0:T(8,128)} custom-call(f32[192,256]{1,0:T(8,128)} %get-tuple-element.16.grads), custom_call_target="tpu_custom_call" | custom-call | tf_op jit(solution)/shard_map/gradsum/pallas_call | solution.py:492
  61.1 2.2 %update.1 = (f32[64,73]{1,0:T(8,128)}, f32[64,577]{1,0:T(8,128)}, f32[32,65]{1,0:T(8,128)}) custom-call(f32[192,256]{1,0:T(8,128)} %gradsum.1.grads, f32[64,73]{1,0:T(8,128)} %d1.1, f32[64,577]{1,0:T(8,128)} %d2.1, f32[32,65]{1,0:T(8,128)} %d3.1, s32[1,160]{1,0:T(1,128)} %bitcast.1), custom_call_target="tpu_custom_call" | custom-call | tf_op jit(solution)/shard_map/update/pallas_call | solution.py:508
where the time goes:
time: 63.5 us; the launch traced here: 63.3 us
  Pallas kernels  62.6 us (99%)
  between operations  0.65 us (1%)
    pallas_call x1, Pallas kernels, per_device(): pl.pallas_call(functools.partial(compute_kernel, sizes), name='local', ou...  29.2 us
    pallas_call x1, Pallas kernels, per_device(): pl.pallas_call(functools.partial(sum_kernel, sizes), name='gradsum', out_...  20.2 us
    pallas_call x1, Pallas kernels, per_device(): pl.pallas_call(functools.partial(halo_kernel, sizes), name='halo', out_sh...  11 us
    pallas_call x1, Pallas kernels, per_device(): pl.pallas_call(finish_kernel, name='update', out_shape=[shape(conv_one.sh...  2.19 us

commit v1 on v0

--- a/solution.py
+++ b/solution.py
@@ -11,6 +11,7 @@
 GROUPS = 6
 PARAMS = 43680
 RIM = 6
+NEAR = 2
 LEV = 8
 C = 64
 K = 32
@@ -35,33 +36,51 @@
     return 0.5 * jnp.tanh(0.5 * v) + 0.5
 
 
-def halo_kernel(sizes, field, target, mask, own, left, right, send_sem, recv_sem):
+def halo_kernel(sizes, field, target, mask, fld, tgt, wet, left, right, packed, send_sem, recv_sem):
     n_gx, n_gy = sizes
     gx = lax.axis_index("gx")
     gy = lax.axis_index("gy")
     h, width = mask.shape
+    lane = lax.broadcasted_iota(jnp.int32, (3 * LEV, TILE), 1)
+    strips = [jnp.zeros((3 * LEV, TILE), F32) for _ in range(2)]
     for r in range(h):
-        wet = jnp.broadcast_to(mask[r : r + 1, :].astype(F32), (LEV, width))
-        own[RIM + r, 0:8, :] = wet * field[:, r, :]
-        own[RIM + r, 8:16, :] = wet
-        own[RIM + r, 16:24, :] = target[:, r, :]
-
-    middle = pl.ds(RIM, h)
-    top = pl.ds(0, RIM)
-    bottom = pl.ds(RIM + h, RIM)
-    first = pl.ds(RIM, RIM)
-    last = pl.ds(h, RIM)
-    all_lanes = pl.ds(0, width)
-    low = pl.ds(0, TILE)
-    high = pl.ds(width - TILE, TILE)
-    rows_of = {1: (last, top), 0: (middle, middle), -1: (first, bottom)}
-    lanes_of = {1: (high, left, low), 0: (all_lanes, own, all_lanes), -1: (low, right, low)}
+        wide_wet = jnp.broadcast_to(mask[r : r + 1, :].astype(F32), (LEV, width))
+        values = wide_wet * field[:, r, :]
+        goal = target[:, r, :]
+        fld[RIM + r] = values
+        tgt[NEAR + r] = goal
+        rows = jnp.concatenate([values, wide_wet, goal], axis=0)
+        here = (lane >= LEV * r) & (lane < LEV * r + LEV)
+        low = rows[:, :TILE]
+        high = rows[:, width - TILE :]
+        strips[0] = jnp.where(here, roll(high, LEV * r + LEV), strips[0])
+        strips[1] = jnp.where(here, roll(low, LEV * r), strips[1])
+    wet[1] = mask[...].astype(F32)
+    packed[0] = strips[0]
+    packed[1] = strips[1]
+
     moves = [(dx, dy) for dx in (-1, 0, 1) for dy in (-1, 0, 1) if (dx, dy) != (0, 0)]
 
     def exists(dx, dy):
         x = gx + dx
         y = gy + dy
         return (x >= 0) & (x < n_gx) & (y >= 0) & (y < n_gy)
+
+    def pairs(dx, dy):
+        if dy:
+            side = left if dy > 0 else right
+            return [(packed.at[0 if dy > 0 else 1], side.at[1 - dx])]
+        if dx > 0:
+            return [
+                (fld.at[pl.ds(h, RIM)], fld.at[pl.ds(0, RIM)]),
+                (tgt.at[pl.ds(h, NEAR)], tgt.at[pl.ds(0, NEAR)]),
+                (wet.at[1], wet.at[0]),
+            ]
+        return [
+            (fld.at[pl.ds(RIM, RIM)], fld.at[pl.ds(RIM + h, RIM)]),
+            (tgt.at[pl.ds(NEAR, NEAR)], tgt.at[pl.ds(NEAR + h, NEAR)]),
+            (wet.at[1], wet.at[2]),
+        ]
 
     barrier = pltpu.get_barrier_semaphore()
     count = jnp.int32(0)
@@ -73,37 +92,42 @@
     for dx, dy in moves:
         @pl.when(jnp.logical_not(exists(-dx, -dy)))
         def _():
-            _, dst_rows = rows_of[dx]
-            _, dst, dst_lanes = lanes_of[dy]
-            dst[dst_rows, :, dst_lanes] = jnp.zeros((dst_rows.size, 24, dst_lanes.size), F32)
+            for _, dst in pairs(dx, dy):
+                dst[...] = jnp.zeros(dst.shape, F32)
     pl.semaphore_wait(barrier, count)
 
     copies = []
-    for index, (dx, dy) in enumerate(moves):
-        src_rows, dst_rows = rows_of[dx]
-        src_lanes, dst, dst_lanes = lanes_of[dy]
-        copies.append(
-            pltpu.make_async_remote_copy(
-                src_ref=own.at[src_rows, :, src_lanes],
-                dst_ref=dst.at[dst_rows, :, dst_lanes],
-                send_sem=send_sem.at[index],
-                recv_sem=recv_sem.at[index],
-                device_id=(gx + dx, gy + dy),
-                device_id_type=MESH,
+    index = 0
+    for dx, dy in moves:
+        group = []
+        for src, dst in pairs(dx, dy):
+            group.append(
+                pltpu.make_async_remote_copy(
+                    src_ref=src,
+                    dst_ref=dst,
+                    send_sem=send_sem.at[index],
+                    recv_sem=recv_sem.at[index],
+                    device_id=(gx + dx, gy + dy),
+                    device_id_type=MESH,
+                )
             )
-        )
-    for (dx, dy), copy in zip(moves, copies):
+            index += 1
+        copies.append((dx, dy, group))
+    for dx, dy, group in copies:
         @pl.when(exists(dx, dy))
         def _():
-            copy.start()
-    for (dx, dy), copy in zip(moves, copies):
+            for copy in group:
+                copy.start()
+    for dx, dy, group in copies:
         @pl.when(exists(-dx, -dy))
         def _():
-            copy.wait_recv()
-    for (dx, dy), copy in zip(moves, copies):
+            for copy in group:
+                copy.wait_recv()
+    for dx, dy, group in copies:
         @pl.when(exists(dx, dy))
         def _():
-            copy.wait_send()
+            for copy in group:
+                copy.wait_send()
 
 
 def roll(v, shift):
@@ -111,7 +135,7 @@
 
 
 def compute_kernel(
-    sizes, own, left, right, w1_ref, w2_ref, w3_ref,
+    sizes, own, goal, mask, left, right, w1_ref, w2_ref, w3_ref,
     final_ref, grads_ref,
     fld, wet_s, tgt, adj, x9, z1, h1, z2, h2, prob, e2m, up, e1m, vv, e3m,
 ):
@@ -122,19 +146,19 @@
     h = rows - 2 * RIM
     wide = width + TILE
 
-    lane = lax.broadcasted_iota(jnp.int32, (LEV, TILE), 1)
-    is_right = lane < TILE // 2
-
-    def merge(r, _):
-        rest = jnp.where(is_right, right[r, 0:8, :], left[r, 0:8, :])
-        fld[0, r] = jnp.concatenate([own[r, 0:8, :], rest], axis=1)
-        rest = jnp.where(is_right, right[r, 8:16, :], left[r, 8:16, :])
-        wet_s[r] = jnp.concatenate([own[r, 8:16, :], rest], axis=1)
-        rest = jnp.where(is_right, right[r, 16:24, :], left[r, 16:24, :])
-        tgt[r] = jnp.concatenate([own[r, 16:24, :], rest], axis=1)
-        return 0
-
-    lax.fori_loop(0, rows, merge, 0)
+    is_right = lax.broadcasted_iota(jnp.int32, (3 * LEV, TILE), 1) < TILE // 2
+
+    for r in range(rows):
+        where = 0 if r < RIM else 1 if r < RIM + h else 2
+        k = (r + h - RIM) % h
+        rest = jnp.where(
+            is_right, roll(right[where], -LEV * k), roll(left[where], -LEV * k - LEV)
+        )
+        fld[0, r] = jnp.concatenate([own[r], rest[:LEV]], axis=1)
+        wet_row = jnp.broadcast_to(mask[where, k : k + 1, :], (LEV, width))
+        wet_s[r] = jnp.concatenate([wet_row, rest[LEV : 2 * LEV]], axis=1)
+        if RIM - NEAR <= r < RIM + h + NEAR:
+            tgt[r] = jnp.concatenate([goal[r - RIM + NEAR], rest[2 * LEV :]], axis=1)
 
     wa = w1_ref[...]
     w1 = wa[:, : 9 * LEV].astype(BF16)
@@ -163,8 +187,8 @@
         ok = (i >= 0) & (i < n_gx * h)
         return col_ok * jnp.where(ok, 1.0, 0.0).astype(F32)
 
-    def loop(start, stop, body, unroll):
-        lax.fori_loop(start, stop, lambda r, c: (body(r), c)[1], 0, unroll=unroll)
+    def loop(start, stop, body):
+        lax.fori_loop(start, stop, lambda r, c: (body(r), c)[1], 0, unroll=True)
 
     def forward(s, rad):
         def first(r):
@@ -178,7 +202,7 @@
             z1[s, r] = z
             h1[s, r] = (z * sigmoid(z) * inside(r)).astype(BF16)
 
-        loop(RIM - rad - 1, RIM + h + rad + 1, first, 2)
+        loop(RIM - rad - 1, RIM + h + rad + 1, first)
 
         def second(r):
             h3 = jnp.concatenate([h1[s, r - 1], h1[s, r], h1[s, r + 1]], axis=0)
@@ -199,7 +223,7 @@
             )
             fld[s + 1, r] = center + wet_s[r] * change
 
-        loop(RIM - rad, RIM + h + rad, second, 2)
+        loop(RIM - rad, RIM + h + rad, second)
 
     forward(0, 4)
     forward(1, 2)
@@ -209,7 +233,7 @@
     def adjoint_start(r):
         adj[1, r] = wet_s[r] * (fld[2, r] - tgt[r])
 
-    loop(RIM - 2, RIM + h + 2, adjoint_start, 1)
+    loop(RIM - 2, RIM + h + 2, adjoint_start)
 
     lane_w = lax.broadcasted_iota(jnp.int32, (1, wide), 1)
     own_lane = jnp.where(lane_w < width, 1.0, 0.0).astype(F32)
@@ -253,7 +277,7 @@
                 up[r] = dot(w2t, spread(e2))
             return (c[0] + fold(e3[:, :width]), c[1] + fold(e2[:, :width]))
 
-        return lax.fori_loop(RIM, RIM + h, body, carry, unroll=2)
+        return lax.fori_loop(RIM, RIM + h, body, carry, unroll=True)
 
     def rim_row(r):
         _, _, e2 = errors(1, r)
@@ -281,7 +305,7 @@
         return c + fold(e1[:, :width]) * keep
 
     sum_one = lax.fori_loop(
-        RIM - 1, RIM + h + 1, back_one, jnp.zeros((C, TILE), F32), unroll=2
+        RIM - 1, RIM + h + 1, back_one, jnp.zeros((C, TILE), F32), unroll=True
     )
 
     def adjoint_next(r):
@@ -302,7 +326,7 @@
             + vv[r - 1, 2]
         )
 
-    loop(RIM, RIM + h, adjoint_next, 1)
+    loop(RIM, RIM + h, adjoint_next)
 
     sums = own_rows(0, sums)
     for r in (RIM - 2, RIM - 1, RIM + h, RIM + h + 1):
@@ -313,7 +337,7 @@
         e1m[0, r - RIM + 1] = e1.astype(BF16)
         return c + fold(e1)
 
-    sum_one = lax.fori_loop(RIM - 1, RIM + h + 1, back_zero, sum_one, unroll=2)
+    sum_one = lax.fori_loop(RIM - 1, RIM + h + 1, back_zero, sum_one, unroll=True)
 
     g1 = jnp.zeros((C, 9 * LEV), F32)
     g2 = jnp.zeros((3 * C, 3 * C), F32)
@@ -450,24 +474,30 @@
     wide = width + TILE
     shape = jax.ShapeDtypeStruct
     chunk = 8 * -(-3 * C // (8 * n_gy))
-    own, left, right = pl.pallas_call(
+    own, goal, wet, left, right = pl.pallas_call(
         functools.partial(halo_kernel, sizes),
         name="halo",
         out_shape=[
-            shape((rows, 24, width), F32),
-            shape((rows, 24, TILE), F32),
-            shape((rows, 24, TILE), F32),
+            shape((rows, LEV, width), F32),
+            shape((h + 2 * NEAR, LEV, width), F32),
+            shape((3, h, width), F32),
+            shape((3, 3 * LEV, TILE), F32),
+            shape((3, 3 * LEV, TILE), F32),
         ],
         in_specs=[VM] * 3,
-        out_specs=[VM] * 3,
-        scratch_shapes=[pltpu.SemaphoreType.DMA((8,)), pltpu.SemaphoreType.DMA((8,))],
+        out_specs=[VM] * 5,
+        scratch_shapes=[
+            pltpu.VMEM((2, 3 * LEV, TILE), F32),
+            pltpu.SemaphoreType.DMA((12,)),
+            pltpu.SemaphoreType.DMA((12,)),
+        ],
         compiler_params=pltpu.CompilerParams(collective_id=0, has_side_effects=True),
     )(field, target, mask)
     final, grads = pl.pallas_call(
         functools.partial(compute_kernel, sizes),
         name="local",
         out_shape=[shape(field.shape, F32), shape((chunk * n_gy, 4 * C), F32)],
-        in_specs=[VM] * 6,
+        in_specs=[VM] * 8,
         out_specs=[VM] * 2,
         scratch_shapes=[
             pltpu.VMEM((3, rows, LEV, wide), F32),
@@ -487,7 +517,7 @@
             pltpu.VMEM((2, h, K, width), BF16),
         ],
         compiler_params=pltpu.CompilerParams(vmem_limit_bytes=LIMIT),
-    )(own, left, right, conv_one, conv_two, head)
+    )(own, goal, wet, left, right, conv_one, conv_two, head)
     dma = pltpu.SemaphoreType.DMA
     summed = pl.pallas_call(
         functools.partial(sum_kernel, sizes),

time: 63.5 us -> 49.5 us (0.78)
  Pallas kernels: 62.6 us -> 48.6 us
    pallas_call x1, Pallas kernels: 29.2 us -> 19.5 us  [per_device(): pl.pallas_call(functools.partial(compute_kernel, sizes), name='local', ou...]
    pallas_call x1, Pallas kernels: 20.2 us -> 17.6 us  [per_device(): pl.pallas_call(functools.partial(sum_kernel, sizes), name='gradsum', out_...]
    pallas_call x1, Pallas kernels: 11 us -> 9.35 us  [per_device(): pl.pallas_call(functools.partial(halo_kernel, sizes), name='halo', out_sh...]
where the time goes in v1:
time: 49.5 us; the launch traced here: 49.3 us
  Pallas kernels  48.6 us (98%)
  between operations  0.65 us (1%)
    pallas_call x1, Pallas kernels, per_device(): pl.pallas_call(functools.partial(compute_kernel, sizes), name='local', ou...  19.5 us
    pallas_call x1, Pallas kernels, per_device(): pl.pallas_call(functools.partial(sum_kernel, sizes), name='gradsum', out_...  17.6 us
    pallas_call x1, Pallas kernels, per_device(): pl.pallas_call(functools.partial(halo_kernel, sizes), name='halo', out_sh...  9.35 us
    pallas_call x1, Pallas kernels, per_device(): pl.pallas_call(finish_kernel, name='update', out_shape=[shape(conv_one.sh...  2.19 us

profile of v1, /device:TPU:0, one launch (start us, length us, event | category | flops | bytes accessed | tf_op | source)
XLA Modules:
  0.0 49.3 jit_solution(12782961995519433242)
XLA Ops:
  0.6 9.3 %halo.1 = (f32[20,8,256]{2,1,0:T(8,128)}, f32[12,8,256]{2,1,0:T(8,128)}, f32[3,8,256]{2,1,0:T(8,128)}, f32[3,24,128]{2,1,0:T(8,128)}, f32[3,24,128]{2,1,0:T(8,128)}) custom-call(f32[8,8,256]{2,1,0:T(8,128)} %field.1, f32[8,8,256]{2,1,0:T(8,128)} %target.1, s32[8,256]{1,0:T(8,128)} %mask.1), custom_call_target="tpu_custom_call" | custom-call | tf_op jit(solution)/shard_map/halo/pallas_call | solution.py:477
  10.0 19.5 %local.1 = (f32[8,8,256]{2,1,0:T(8,128)}, f32[192,256]{1,0:T(8,128)}) custom-call(f32[20,8,256]{2,1,0:T(8,128)} %get-tuple-element.14.own, f32[12,8,256]{2,1,0:T(8,128)} %get-tuple-element.15.goal, f32[3,8,256]{2,1,0:T(8,128)} %get-tuple-element.16.mask, f32[3,24,128]{2,1,0:T(8,128)} %get-tuple-element.17.left, f32[3,24,128]{2,1,0:T(8,128)} %get-tuple-element.18.right, ...), custom_call_target="tpu_custom_call" | custom-call | tf_op jit(solution)/shard_map/local/pallas_call | solution.py:496
  29.4 17.6 %gradsum.1.grads = f32[192,256]{1,0:T(8,128)} custom-call(f32[192,256]{1,0:T(8,128)} %get-tuple-element.20.grads), custom_call_target="tpu_custom_call" | custom-call | tf_op jit(solution)/shard_map/gradsum/pallas_call | solution.py:522
  47.1 2.2 %update.1 = (f32[64,73]{1,0:T(8,128)}, f32[64,577]{1,0:T(8,128)}, f32[32,65]{1,0:T(8,128)}) custom-call(f32[192,256]{1,0:T(8,128)} %gradsum.1.grads, f32[64,73]{1,0:T(8,128)} %d1.1, f32[64,577]{1,0:T(8,128)} %d2.1, f32[32,65]{1,0:T(8,128)} %d3.1, s32[1,160]{1,0:T(1,128)} %bitcast.1), custom_call_target="tpu_custom_call" | custom-call | tf_op jit(solution)/shard_map/update/pallas_call | solution.py:538

commit v2 on v1

--- a/solution.py
+++ b/solution.py
@@ -202,7 +202,6 @@
             z1[s, r] = z
             h1[s, r] = (z * sigmoid(z) * inside(r)).astype(BF16)
 
-        loop(RIM - rad - 1, RIM + h + rad + 1, first)
 
         def second(r):
             h3 = jnp.concatenate([h1[s, r - 1], h1[s, r], h1[s, r + 1]], axis=0)
@@ -223,7 +222,14 @@
             )
             fld[s + 1, r] = center + wet_s[r] * change
 
-        loop(RIM - rad, RIM + h + rad, second)
+        begin = RIM - rad
+        first(begin - 1)
+        first(begin)
+        first(begin + 1)
+        for r in range(begin, RIM + h + rad):
+            if r + 2 <= RIM + h + rad:
+                first(r + 2)
+            second(r)
 
     forward(0, 4)
     forward(1, 2)
@@ -264,7 +270,7 @@
 
     zero_b = (jnp.zeros((K, TILE), F32), jnp.zeros((C, TILE), F32))
 
-    def own_rows(s, carry):
+    def own_row(s):
         def body(r, c):
             e3, e3b, e2 = errors(s, r)
             e3m[s, r - RIM] = e3b[:, :width]
@@ -277,7 +283,7 @@
                 up[r] = dot(w2t, spread(e2))
             return (c[0] + fold(e3[:, :width]), c[1] + fold(e2[:, :width]))
 
-        return lax.fori_loop(RIM, RIM + h, body, carry, unroll=True)
+        return body
 
     def rim_row(r):
         _, _, e2 = errors(1, r)
@@ -288,10 +294,6 @@
         z = z1[s, r]
         g = sigmoid(z)
         return hid * (g * (1.0 + z * (1.0 - g))) * inside(r)
-
-    sums = own_rows(1, zero_b)
-    for r in (RIM - 2, RIM - 1, RIM + h, RIM + h + 1):
-        rim_row(r)
 
     def back_one(r, c):
         e1 = first_error(1, r)
@@ -301,12 +303,19 @@
         piece = lambda a, b: t[(3 * a + b) * LEV : (3 * a + b + 1) * LEV]
         for a in range(3):
             vv[r, a] = roll(piece(a, 0), -1) + piece(a, 1) + roll(piece(a, 2), 1)
-        keep = jnp.where((r >= RIM) & (r < RIM + h), 1.0, 0.0).astype(F32)
-        return c + fold(e1[:, :width]) * keep
-
-    sum_one = lax.fori_loop(
-        RIM - 1, RIM + h + 1, back_one, jnp.zeros((C, TILE), F32), unroll=True
-    )
+        return c + fold(e1[:, :width]) if RIM <= r < RIM + h else c
+
+    def backward(rim, own_part, back, sums, sum_one):
+        for r in range(RIM - 2, RIM + h + 2):
+            if RIM <= r < RIM + h:
+                sums = own_part(r, sums)
+            else:
+                rim(r)
+            if r >= RIM:
+                sum_one = back(r - 1, sum_one)
+        return sums, sum_one
+
+    sums, sum_one = backward(rim_row, own_row(1), back_one, zero_b, jnp.zeros((C, TILE), F32))
 
     def adjoint_next(r):
         wg = wet_s[r] * adj[1, r]
@@ -328,8 +337,7 @@
 
     loop(RIM, RIM + h, adjoint_next)
 
-    sums = own_rows(0, sums)
-    for r in (RIM - 2, RIM - 1, RIM + h, RIM + h + 1):
+    def rim_zero(r):
         up[r] = jnp.zeros((3 * C, wide), F32)
 
     def back_zero(r, c):
@@ -337,7 +345,7 @@
         e1m[0, r - RIM + 1] = e1.astype(BF16)
         return c + fold(e1)
 
-    sum_one = lax.fori_loop(RIM - 1, RIM + h + 1, back_zero, sum_one, unroll=True)
+    sums, sum_one = backward(rim_zero, own_row(0), back_zero, sums, sum_one)
 
     g1 = jnp.zeros((C, 9 * LEV), F32)
     g2 = jnp.zeros((3 * C, 3 * C), F32)

time: 49.5 us -> 49.9 us (level)
  Pallas kernels: 48.6 us -> 49.1 us
where the time goes in v2:
time: 49.9 us; the launch traced here: 49.7 us
  Pallas kernels  49.1 us (98%)
  between operations  0.65 us (1%)
    pallas_call x1, Pallas kernels, per_device(): pl.pallas_call(functools.partial(compute_kernel, sizes), name='local', ou...  19.9 us
    pallas_call x1, Pallas kernels, per_device(): pl.pallas_call(functools.partial(sum_kernel, sizes), name='gradsum', out_...  17.6 us
    pallas_call x1, Pallas kernels, per_device(): pl.pallas_call(functools.partial(halo_kernel, sizes), name='halo', out_sh...  9.35 us
    pallas_call x1, Pallas kernels, per_device(): pl.pallas_call(finish_kernel, name='update', out_shape=[shape(conv_one.sh...  2.19 us

profile of v2, /device:TPU:0, one launch (start us, length us, event | category | flops | bytes accessed | tf_op | source)
XLA Modules:
  0.0 49.7 jit_solution(5278835510662453960)
XLA Ops:
  0.6 9.3 %halo.1 = (f32[20,8,256]{2,1,0:T(8,128)}, f32[12,8,256]{2,1,0:T(8,128)}, f32[3,8,256]{2,1,0:T(8,128)}, f32[3,24,128]{2,1,0:T(8,128)}, f32[3,24,128]{2,1,0:T(8,128)}) custom-call(f32[8,8,256]{2,1,0:T(8,128)} %field.1, f32[8,8,256]{2,1,0:T(8,128)} %target.1, s32[8,256]{1,0:T(8,128)} %mask.1), custom_call_target="tpu_custom_call" | custom-call | tf_op jit(solution)/shard_map/halo/pallas_call | solution.py:485
  10.0 19.9 %local.1 = (f32[8,8,256]{2,1,0:T(8,128)}, f32[192,256]{1,0:T(8,128)}) custom-call(f32[20,8,256]{2,1,0:T(8,128)} %get-tuple-element.14.own, f32[12,8,256]{2,1,0:T(8,128)} %get-tuple-element.15.goal, f32[3,8,256]{2,1,0:T(8,128)} %get-tuple-element.16.mask, f32[3,24,128]{2,1,0:T(8,128)} %get-tuple-element.17.left, f32[3,24,128]{2,1,0:T(8,128)} %get-tuple-element.18.right, ...), custom_call_target="tpu_custom_call" | custom-call | tf_op jit(solution)/shard_map/local/pallas_call | solution.py:504
  29.9 17.6 %gradsum.1.grads = f32[192,256]{1,0:T(8,128)} custom-call(f32[192,256]{1,0:T(8,128)} %get-tuple-element.20.grads), custom_call_target="tpu_custom_call" | custom-call | tf_op jit(solution)/shard_map/gradsum/pallas_call | solution.py:530
  47.5 2.2 %update.1 = (f32[64,73]{1,0:T(8,128)}, f32[64,577]{1,0:T(8,128)}, f32[32,65]{1,0:T(8,128)}) custom-call(f32[192,256]{1,0:T(8,128)} %gradsum.1.grads, f32[64,73]{1,0:T(8,128)} %d1.1, f32[64,577]{1,0:T(8,128)} %d2.1, f32[32,65]{1,0:T(8,128)} %d3.1, s32[1,160]{1,0:T(1,128)} %bitcast.1), custom_call_target="tpu_custom_call" | custom-call | tf_op jit(solution)/shard_map/update/pallas_call | solution.py:546
